TPU v7x, 32 devices: a whole 2x2x4 slice. The times are simulated.
32 devices in a mesh: prow: 4 (over y, core), pcol: 8 (over z, x).
Axes of the slice: x: 2, y: 2, z: 4, core: 2. Of those that a mesh axis runs over, the one named last changes fastest.
Arguments:
- right_side: float32 [8, 256, 128], P(None, 'prow'), may hold values from -6 to 6
- lower_prev: float32 [8, 256, 129024], P(None, 'prow', 'pcol'), may hold values from -0.015625 to 0.015625
- solved_prev: float32 [129024, 128], P('pcol'), may hold values from -6 to 6
- lower_window: float32 [8, 256, 2048], P(None, 'prow', 'pcol'), may hold values from -0.1875 to 0.1875
- inverse_diag: float32 [8, 256, 256], P(None, 'prow'), may hold values from -0.25 to 1.4, as said below
Outputs:
- solution: float32 [8, 256, 128], P(None, 'prow')
Inputs may be any that keep to these rules, and one draw needn't show every extreme that they name: `inverse_diag`: each block is lower triangular: zero above its diagonal, with diagonal entries of 0.7 to 1.4.
All inputs are finite; a program needn't handle non-finite values.
Results may differ from a plain program's by a relative error of at most 0.00011.
Values sent between devices are 32-bit elements; how exact they have to be, the bound alone decides.
No kernel may reach another device: no remote copies, remote signals or barrier semaphores. Data moves between devices by JAX's collectives and lax.ppermute only.
A program may use at most 128 MiB of HBM per device.

v0:
```python
import jax
import jax.numpy as jnp
from jax import lax
from jax.sharding import PartitionSpec as P


def local(right_side, lower_prev, solved_prev, lower_window, inverse_diag):
    highest = lax.Precision.HIGHEST
    blocks = right_side.shape[0]
    local_rows = right_side.shape[1]
    columns = right_side.shape[2]
    block_rows = inverse_diag.shape[2]
    row_start = lax.axis_index("prow") * local_rows
    solved = jnp.zeros((blocks * block_rows, columns), jnp.float32)
    pieces = []
    full_inverse = lax.all_gather(inverse_diag, "prow", axis=1, tiled=True)
    full_window = lax.all_gather(lower_window, "pcol", axis=2, tiled=True)
    for row_block in range(blocks):
        window_term = jnp.dot(
            full_window[row_block], solved, precision=highest, preferred_element_type=jnp.float32
        )
        earlier_part = jnp.dot(
            lower_prev[row_block],
            solved_prev,
            precision=highest,
            preferred_element_type=jnp.float32,
        )
        earlier_here = lax.psum(earlier_part, "pcol")
        local_residual = right_side[row_block] - (earlier_here + window_term)
        residual = lax.all_gather(local_residual, "prow", axis=0, tiled=True)
        whole_rows = jnp.dot(
            full_inverse[row_block], residual, precision=highest, preferred_element_type=jnp.float32
        )
        pieces.append(lax.dynamic_slice_in_dim(whole_rows, row_start, local_rows, 0))
        solved = lax.dynamic_update_slice_in_dim(solved, whole_rows, row_block * block_rows, 0)
    return jnp.stack(pieces)


def solution(mesh):
    in_specs = (
        P(None, "prow", None),
        P(None, "prow", "pcol"),
        P("pcol", None),
        P(None, "prow", "pcol"),
        P(None, "prow", None),
    )
    out_specs = P(None, "prow", None)
    return jax.shard_map(local, mesh=mesh, in_specs=in_specs, out_specs=out_specs, check_vma=False)
```

profile of v0, /device:TPU:0, one launch (start us, length us, event | category | flops | bytes accessed | tf_op | source)
XLA Modules:
  0.0 249.5 jit_solution(15784132453054589347)
XLA Ops:
  7.3 10.3 %fusion.4 = f32[64,128]{1,0:T(8,128)} fusion(f32[16128,128]{1,0:T(8,128)} %param.7, f32[8,64,16128]{2,1,0:T(8,128)} %param.6), kind=kOutput, calls=%fused_computation.4 | convolution fusion | flops 1585446912 | bytes 12419072 | tf_op jit(solution)/shard_map/dot_general | solution.py:22
  17.7 8.1 %fusion.6 = f32[64,128]{1,0:T(8,128)} fusion(f32[16128,128]{1,0:T(8,128)S(1)} %copy-done, f32[8,64,16128]{2,1,0:T(8,128)} %param.6), kind=kOutput, calls=%fused_computation.6 | convolution fusion | flops 1585446912 | bytes 12419072 | tf_op jit(solution)/shard_map/dot_general | solution.py:22
  25.8 7.9 %fusion.8 = f32[64,128]{1,0:T(8,128)} fusion(f32[16128,128]{1,0:T(8,128)S(1)} %copy-done, f32[8,64,16128]{2,1,0:T(8,128)} %param.6), kind=kOutput, calls=%fused_computation.8 | convolution fusion | flops 1585446912 | bytes 12419072 | tf_op jit(solution)/shard_map/dot_general | solution.py:22
  33.7 8.1 %fusion.10 = f32[64,128]{1,0:T(8,128)} fusion(f32[16128,128]{1,0:T(8,128)S(1)} %copy-done, f32[8,64,16128]{2,1,0:T(8,128)} %param.6), kind=kOutput, calls=%fused_computation.10 | convolution fusion | flops 1585446912 | bytes 12419072 | tf_op jit(solution)/shard_map/dot_general | solution.py:22
  41.8 7.9 %fusion.12 = f32[64,128]{1,0:T(8,128)} fusion(f32[16128,128]{1,0:T(8,128)S(1)} %copy-done, f32[8,64,16128]{2,1,0:T(8,128)} %param.6), kind=kOutput, calls=%fused_computation.12 | convolution fusion | flops 1585446912 | bytes 12419072 | tf_op jit(solution)/shard_map/dot_general | solution.py:22
  49.7 8.4 %fusion.14 = f32[64,128]{1,0:T(8,128)} fusion(f32[16128,128]{1,0:T(8,128)S(1)} %copy-done, f32[8,64,16128]{2,1,0:T(8,128)} %param.6), kind=kOutput, calls=%fused_computation.14 | convolution fusion | flops 1585446912 | bytes 12419072 | tf_op jit(solution)/shard_map/dot_general | solution.py:22
  58.1 7.9 %fusion = f32[64,128]{1,0:T(8,128)} fusion(f32[16128,128]{1,0:T(8,128)S(1)} %copy-done, f32[8,64,16128]{2,1,0:T(8,128)} %param.6), kind=kOutput, calls=%fused_computation | convolution fusion | flops 1585446912 | bytes 12419072 | tf_op jit(solution)/shard_map/dot_general | solution.py:22
  66.1 8.2 %fusion.2 = f32[64,128]{1,0:T(8,128)} fusion(f32[16128,128]{1,0:T(8,128)S(1)} %copy-done, f32[8,64,16128]{2,1,0:T(8,128)} %param.6), kind=kOutput, calls=%fused_computation.2 | convolution fusion | flops 1585446912 | bytes 12419072 | tf_op jit(solution)/shard_map/dot_general | solution.py:22
  75.0 12.2 %all-gather.3.cloned.1.call-done = f32[8,64,2048]{2,1,0:T(8,128)} async-done(((f32[8,64,256]{2,1,0:T(8,128)}), f32[8,64,2048]{2,1,0:T(8,128)}) %all-gather.3.cloned.1.call-update) | async-done | bytes 4194320 | tf_op jit(solution)/shard_map/all_gather | solution.py:17
  88.3 73.8 %all-reduce.4.cloned.1.call-done = (f32[64,128]{1,0:T(8,128)}, f32[64,128]{1,0:T(8,128)}, f32[64,128]{1,0:T(8,128)}, f32[64,128]{1,0:T(8,128)}, f32[64,128]{1,0:...) async-done(((f32[64,128]{1,0:T(8,128)}, f32[64,128]{1,0:T(8,128)}, f32[64,128]{1,0:T(8,128)}, f32[64,128]{1,0:T(8,128)}, f32[64,128]{1,0:T(8,128)}, ...) | async-done | bytes 262160 | tf_op jit(solution)/shard_map/psum | solution.py:28
  163.0 5.4 %all_gather.31 = f32[256,128]{1,0:T(8,128)S(1)} all-gather(f32[64,128]{1,0:T(8,128)S(1)} %bitcast_subtract_fusion), channel_id=1, replica_groups=mesh['prow'=4,'pcol'=8] {'prow'}, dimensions={0}, use_global_device_ids=true | all-gather | bytes 163840 | tf_op jit(solution)/shard_map/all_gather | solution.py:30
  168.4 17.4 %all-gather.5.cloned.1.call-done = f32[8,256,256]{2,1,0:T(8,128)} async-done(((f32[8,64,256]{2,1,0:T(8,128)}), f32[8,256,256]{2,1,0:T(8,128)}) %all-gather.5.cloned.1.call-update) | async-done | bytes 2097168 | tf_op jit(solution)/shard_map/all_gather | solution.py:16
  185.8 1.5 fusion.47
  187.3 2.1 fusion.25
  189.4 5.4 %all_gather.33 = f32[256,128]{1,0:T(8,128)S(1)} all-gather(f32[64,128]{1,0:T(8,128)S(1)} %fusion.25), channel_id=1, replica_groups=mesh['prow'=4,'pcol'=8] {'prow'}, dimensions={0}, use_global_device_ids=true | all-gather | bytes 163840 | tf_op jit(solution)/shard_map/all_gather | solution.py:30
  195.0 1.4 bitcast_dynamic-update-slice_fusion.5
  196.4 2.3 fusion.27
  198.7 5.4 %all_gather.34 = f32[256,128]{1,0:T(8,128)S(1)} all-gather(f32[64,128]{1,0:T(8,128)S(1)} %fusion.27), channel_id=1, replica_groups=mesh['prow'=4,'pcol'=8] {'prow'}, dimensions={0}, use_global_device_ids=true | all-gather | bytes 163840 | tf_op jit(solution)/shard_map/all_gather | solution.py:30
  204.1 1.4 bitcast_dynamic-update-slice_fusion.4
  206.7 5.6 %all_gather.35 = f32[256,128]{1,0:T(8,128)S(1)} all-gather(f32[64,128]{1,0:T(8,128)S(1)} %fusion.29), channel_id=1, replica_groups=mesh['prow'=4,'pcol'=8] {'prow'}, dimensions={0}, use_global_device_ids=true | all-gather | bytes 163840 | tf_op jit(solution)/shard_map/all_gather | solution.py:30
  213.9 5.4 %all_gather.36 = f32[256,128]{1,0:T(8,128)S(1)} all-gather(f32[64,128]{1,0:T(8,128)S(1)} %fusion.31), channel_id=1, replica_groups=mesh['prow'=4,'pcol'=8] {'prow'}, dimensions={0}, use_global_device_ids=true | all-gather | bytes 163840 | tf_op jit(solution)/shard_map/all_gather | solution.py:30
  221.0 5.4 %all_gather.37 = f32[256,128]{1,0:T(8,128)S(1)} all-gather(f32[64,128]{1,0:T(8,128)S(1)} %fusion.33), channel_id=1, replica_groups=mesh['prow'=4,'pcol'=8] {'prow'}, dimensions={0}, use_global_device_ids=true | all-gather | bytes 163840 | tf_op jit(solution)/shard_map/all_gather | solution.py:30
  228.1 5.6 %all_gather.38 = f32[256,128]{1,0:T(8,128)S(1)} all-gather(f32[64,128]{1,0:T(8,128)S(1)} %fusion.35), channel_id=1, replica_groups=mesh['prow'=4,'pcol'=8] {'prow'}, dimensions={0}, use_global_device_ids=true | all-gather | bytes 163840 | tf_op jit(solution)/shard_map/all_gather | solution.py:30
  235.4 5.4 %all_gather.39 = f32[256,128]{1,0:T(8,128)S(1)} all-gather(f32[64,128]{1,0:T(8,128)S(1)} %fusion.37), channel_id=1, replica_groups=mesh['prow'=4,'pcol'=8] {'prow'}, dimensions={0}, use_global_device_ids=true | all-gather | bytes 163840 | tf_op jit(solution)/shard_map/all_gather | solution.py:30
  (46 shorter events, 13.4 us)
Async XLA Ops:
  6.5 80.6 %all-gather.3.cloned.1.call-start = ((), (), s32[]{:S(2)}) async-start(), calls=%async_computation | async-start | bytes 4718592 | tf_op jit(solution)/shard_map/all_gather | solution.py:17
  7.3 154.9 %all-reduce.4.cloned.1.call-start = ((), (), s32[]{:S(2)}) async-start(), calls=%async_computation.2 | async-start | bytes 524288 | tf_op jit(solution)/shard_map/psum | solution.py:28
  7.3 10.4 %copy-start = (f32[16128,128]{1,0:T(8,128)S(1)}, f32[16128,128]{1,0:T(8,128)}, u32[]{:S(2)}) copy-start(f32[16128,128]{1,0:T(8,128)} %param.7) | copy-start | bytes 24772612
  66.1 96.1 %copy-start.3 = (f32[8,64,128]{2,1,0:T(8,128)S(1)}, f32[8,64,128]{2,1,0:T(8,128)}, u32[]{:S(2)}) copy-start(f32[8,64,128]{2,1,0:T(8,128)} %param.5) | copy-start | bytes 786436
  74.2 111.6 %all-gather.5.cloned.1.call-start = ((), (), s32[]{:S(2)}) async-start(), calls=%async_computation.1 | async-start | bytes 2621440 | tf_op jit(solution)/shard_map/all_gather | solution.py:16
  162.1 43.4 %copy-start.8 = (f32[64,128]{1,0:T(8,128)S(1)}, f32[64,128]{1,0:T(8,128)}, u32[]{:S(2)}) copy-start(f32[64,128]{1,0:T(8,128)} %get-tuple-element.8) | copy-start | bytes 98308
  168.4 44.3 %copy-start.7 = (f32[64,128]{1,0:T(8,128)S(1)}, f32[64,128]{1,0:T(8,128)}, u32[]{:S(2)}) copy-start(f32[64,128]{1,0:T(8,128)} %get-tuple-element.9) | copy-start | bytes 98308
  185.8 19.7 %copy-start.1 = (f32[8,64,2048]{2,1,0:T(8,128)S(1)}, f32[8,64,2048]{2,1,0:T(8,128)}, u32[]{:S(2)}) copy-start(f32[8,64,2048]{2,1,0:T(8,128)} %all-gather.3.cloned.1.call-done) | copy-start | bytes 12582916
  185.8 26.5 %copy-start.2 = (f32[8,256,256]{2,1,0:T(8,128)S(1)}, f32[8,256,256]{2,1,0:T(8,128)}, u32[]{:S(2)}) copy-start(f32[8,256,256]{2,1,0:T(8,128)} %all-gather.5.cloned.1.call-done) | copy-start | bytes 6291460
  195.0 24.8 %copy-start.6 = (f32[64,128]{1,0:T(8,128)S(1)}, f32[64,128]{1,0:T(8,128)}, u32[]{:S(2)}) copy-start(f32[64,128]{1,0:T(8,128)} %get-tuple-element.10) | copy-start | bytes 98308
  198.7 28.2 %copy-start.5 = (f32[64,128]{1,0:T(8,128)S(1)}, f32[64,128]{1,0:T(8,128)}, u32[]{:S(2)}) copy-start(f32[64,128]{1,0:T(8,128)} %get-tuple-element.11) | copy-start | bytes 98308
  206.7 27.4 %copy-start.4 = (f32[64,128]{1,0:T(8,128)S(1)}, f32[64,128]{1,0:T(8,128)}, u32[]{:S(2)}) copy-start(f32[64,128]{1,0:T(8,128)} %get-tuple-element.12) | copy-start | bytes 98308
Sparse Core Ops, SparseCore 0:
  9.4 77.7 all-gather.2
  91.4 70.6 all-reduce.3
  163.8 21.9 all-gather.4
where the time goes:
time: 253 us; the launch traced here: 249 us
  waiting for transfers between devices  105 us (42%)
  matrix products  83.6 us (33%)
  blocking collectives  43.7 us (17%)
  between operations  13.6 us (5%)
    psum x1, waiting for transfers between devices, local(): earlier_here = lax.psum(earlier_part, 'pcol')  73.8 us
    dot_general x8, matrix products, local(): jnp.dot(lower_prev[row_block], solved_prev, precision=highest, preferred_...  66.9 us
    all_gather x8, blocking collectives, local(): residual = lax.all_gather(local_residual, 'prow', axis=0, tiled=True)  43.7 us
    all_gather x1, waiting for transfers between devices, local(): full_inverse = lax.all_gather(inverse_diag, 'prow', axis=1, tiled=True)  17.4 us
    all_gather x1, waiting for transfers between devices, local(): full_window = lax.all_gather(lower_window, 'pcol', axis=2, tiled=True)  12.2 us
    dot_general x7, matrix products, local(): jnp.dot(full_window[row_block], solved, precision=highest, preferred_elem...  10.4 us
    dot_general x8, matrix products, local(): jnp.dot(full_inverse[row_block], residual, precision=highest, preferred_e...  6.33 us
  transfers between devices with their start and end apart: 3, of which 3 were waited for; matrix products, arithmetic and copies ran while one was open for 28% of the time, Pallas kernels for 0%

commit v1 on v0

--- a/solution.py
+++ b/solution.py
@@ -25,7 +25,7 @@
             precision=highest,
             preferred_element_type=jnp.float32,
         )
-        earlier_here = lax.psum(earlier_part, "pcol")
+        earlier_here = jnp.sum(lax.all_gather(earlier_part, "pcol"), axis=0)
         local_residual = right_side[row_block] - (earlier_here + window_term)
         residual = lax.all_gather(local_residual, "prow", axis=0, tiled=True)
         whole_rows = jnp.dot(

time: 253 us -> 398 us (1.57)
  blocking collectives: 43.7 us -> 294 us
  waiting for transfers between devices: 105 us -> 1.43 us
    all_gather x0 -> x8, blocking collectives: none -> 250 us  [local(): earlier_here = jnp.sum(lax.all_gather(earlier_part, 'pcol'), axis=0)]
    psum x1 -> x0, waiting for transfers between devices: 73.8 us -> none  [local(): earlier_here = lax.psum(earlier_part, 'pcol')]
    all_gather x1, waiting for transfers between devices: 17.4 us -> 0.01 us  [local(): full_inverse = lax.all_gather(inverse_diag, 'prow', axis=1, tiled=True)]
    all_gather x1, waiting for transfers between devices: 12.2 us -> 0.02 us  [local(): full_window = lax.all_gather(lower_window, 'pcol', axis=2, tiled=True)]
  transfers between devices with their start and end apart: 3 -> 2, of which waited for: 3 -> 0; matrix products, arithmetic and copies ran while one was open for 28% -> 17% of each run, Pallas kernels for 0% -> 0%
where the time goes in v1:
time: 398 us; the launch traced here: 395 us
  blocking collectives  294 us (74%)
  matrix products  82.5 us (21%)
  between operations  13.9 us (3%)
    all_gather x8, blocking collectives, local(): earlier_here = jnp.sum(lax.all_gather(earlier_part, 'pcol'), axis=0)  250 us
    dot_general x8, matrix products, local(): jnp.dot(lower_prev[row_block], solved_prev, precision=highest, preferred_...  66 us
    all_gather x8, blocking collectives, local(): residual = lax.all_gather(local_residual, 'prow', axis=0, tiled=True)  43.6 us
    dot_general x7, matrix products, local(): jnp.dot(full_window[row_block], solved, precision=highest, preferred_elem...  10.2 us
  transfers between devices with their start and end apart: 2, of which 0 were waited for; matrix products, arithmetic and copies ran while one was open for 17% of the time, Pallas kernels for 0%

profile of v1, /device:TPU:0, one launch (start us, length us, event | category | flops | bytes accessed | tf_op | source)
XLA Modules:
  0.0 394.9 jit_solution(330838243085122896)
XLA Ops:
  8.0 10.4 %fusion.14 = f32[64,128]{1,0:T(8,128)S(1)} fusion(f32[16128,128]{1,0:T(8,128)} %param.7, f32[8,64,16128]{2,1,0:T(8,128)} %param.6), kind=kOutput, calls=%fused_computation.14 | convolution fusion | flops 1585446912 | bytes 12419072 | tf_op jit(solution)/shard_map/dot_general | solution.py:22
  18.4 7.6 %fusion.12 = f32[64,128]{1,0:T(8,128)S(1)} fusion(f32[16128,128]{1,0:T(8,128)S(1)} %copy-done, f32[8,64,16128]{2,1,0:T(8,128)} %param.6), kind=kOutput, calls=%fused_computation.12 | convolution fusion | flops 1585446912 | bytes 12419072 | tf_op jit(solution)/shard_map/dot_general | solution.py:22
  26.0 7.3 %fusion.10 = f32[64,128]{1,0:T(8,128)S(1)} fusion(f32[16128,128]{1,0:T(8,128)S(1)} %copy-done, f32[8,64,16128]{2,1,0:T(8,128)} %param.6), kind=kOutput, calls=%fused_computation.10 | convolution fusion | flops 1585446912 | bytes 12419072 | tf_op jit(solution)/shard_map/dot_general | solution.py:22
  33.3 7.5 %fusion.8 = f32[64,128]{1,0:T(8,128)S(1)} fusion(f32[16128,128]{1,0:T(8,128)S(1)} %copy-done, f32[8,64,16128]{2,1,0:T(8,128)} %param.6), kind=kOutput, calls=%fused_computation.8 | convolution fusion | flops 1585446912 | bytes 12419072 | tf_op jit(solution)/shard_map/dot_general | solution.py:22
  40.8 33.7 %all-gather = f32[512,128]{1,0:T(8,128)S(1)} all-gather(f32[64,128]{1,0:T(8,128)S(1)} %fusion.14), channel_id=2, replica_groups=mesh['prow'=4,'pcol'=8] {'pcol'}, dimensions={0}, use_global_device_ids=true | all-gather | bytes 294912 | tf_op jit(solution)/shard_map/all_gather | solution.py:28
  74.5 31.7 %all-gather.1 = f32[512,128]{1,0:T(8,128)S(1)} all-gather(f32[64,128]{1,0:T(8,128)S(1)} %fusion.12), channel_id=3, replica_groups=mesh['prow'=4,'pcol'=8] {'pcol'}, dimensions={0}, use_global_device_ids=true | all-gather | bytes 294912 | tf_op jit(solution)/shard_map/all_gather | solution.py:28
  106.3 30.9 %all-gather.2 = f32[512,128]{1,0:T(8,128)S(1)} all-gather(f32[64,128]{1,0:T(8,128)S(1)} %fusion.10), channel_id=4, replica_groups=mesh['prow'=4,'pcol'=8] {'pcol'}, dimensions={0}, use_global_device_ids=true | all-gather | bytes 294912 | tf_op jit(solution)/shard_map/all_gather | solution.py:28
  137.2 30.8 %all-gather.3 = f32[512,128]{1,0:T(8,128)S(1)} all-gather(f32[64,128]{1,0:T(8,128)S(1)} %fusion.8), channel_id=5, replica_groups=mesh['prow'=4,'pcol'=8] {'pcol'}, dimensions={0}, use_global_device_ids=true | all-gather | bytes 294912 | tf_op jit(solution)/shard_map/all_gather | solution.py:28
  168.0 8.2 %fusion.6 = f32[64,128]{1,0:T(8,128)S(1)} fusion(f32[16128,128]{1,0:T(8,128)} %param.7, f32[8,64,16128]{2,1,0:T(8,128)} %param.6), kind=kOutput, calls=%fused_computation.6 | convolution fusion | flops 1585446912 | bytes 12419072 | tf_op jit(solution)/shard_map/dot_general | solution.py:22
  176.3 30.8 %all-gather.4 = f32[512,128]{1,0:T(8,128)S(1)} all-gather(f32[64,128]{1,0:T(8,128)S(1)} %fusion.6), channel_id=6, replica_groups=mesh['prow'=4,'pcol'=8] {'pcol'}, dimensions={0}, use_global_device_ids=true | all-gather | bytes 294912 | tf_op jit(solution)/shard_map/all_gather | solution.py:28
  207.1 8.2 %fusion.4 = f32[64,128]{1,0:T(8,128)S(1)} fusion(f32[16128,128]{1,0:T(8,128)} %param.7, f32[8,64,16128]{2,1,0:T(8,128)} %param.6), kind=kOutput, calls=%fused_computation.4 | convolution fusion | flops 1585446912 | bytes 12419072 | tf_op jit(solution)/shard_map/dot_general | solution.py:22
  215.4 30.9 %all-gather.5 = f32[512,128]{1,0:T(8,128)S(1)} all-gather(f32[64,128]{1,0:T(8,128)S(1)} %fusion.4), channel_id=7, replica_groups=mesh['prow'=4,'pcol'=8] {'pcol'}, dimensions={0}, use_global_device_ids=true | all-gather | bytes 294912 | tf_op jit(solution)/shard_map/all_gather | solution.py:28
  246.3 8.5 %fusion.2 = f32[64,128]{1,0:T(8,128)S(1)} fusion(f32[16128,128]{1,0:T(8,128)} %param.7, f32[8,64,16128]{2,1,0:T(8,128)} %param.6), kind=kOutput, calls=%fused_computation.2 | convolution fusion | flops 1585446912 | bytes 12419072 | tf_op jit(solution)/shard_map/dot_general | solution.py:22
  254.7 30.8 %all-gather.6 = f32[512,128]{1,0:T(8,128)S(1)} all-gather(f32[64,128]{1,0:T(8,128)S(1)} %fusion.2), channel_id=8, replica_groups=mesh['prow'=4,'pcol'=8] {'pcol'}, dimensions={0}, use_global_device_ids=true | all-gather | bytes 294912 | tf_op jit(solution)/shard_map/all_gather | solution.py:28
  285.5 8.3 %fusion = f32[64,128]{1,0:T(8,128)S(1)} fusion(f32[16128,128]{1,0:T(8,128)} %param.7, f32[8,64,16128]{2,1,0:T(8,128)} %param.6), kind=kOutput, calls=%fused_computation | convolution fusion | flops 1585446912 | bytes 12419072 | tf_op jit(solution)/shard_map/dot_general | solution.py:22
  293.8 30.7 %all-gather.7 = f32[512,128]{1,0:T(8,128)S(1)} all-gather(f32[64,128]{1,0:T(8,128)S(1)} %fusion), channel_id=9, replica_groups=mesh['prow'=4,'pcol'=8] {'pcol'}, dimensions={0}, use_global_device_ids=true | all-gather | bytes 294912 | tf_op jit(solution)/shard_map/all_gather | solution.py:28
  325.9 5.4 %all_gather.81 = f32[256,128]{1,0:T(8,128)S(1)} all-gather(f32[64,128]{1,0:T(8,128)S(1)} %bitcast_subtract_fusion), channel_id=1, replica_groups=mesh['prow'=4,'pcol'=8] {'prow'}, dimensions={0}, use_global_device_ids=true | all-gather | bytes 163840 | tf_op jit(solution)/shard_map/all_gather | solution.py:30
  334.9 5.4 %all_gather.85 = f32[256,128]{1,0:T(8,128)S(1)} all-gather(f32[64,128]{1,0:T(8,128)S(1)} %fusion.25), channel_id=1, replica_groups=mesh['prow'=4,'pcol'=8] {'prow'}, dimensions={0}, use_global_device_ids=true | all-gather | bytes 163840 | tf_op jit(solution)/shard_map/all_gather | solution.py:30
  343.9 5.4 %all_gather.88 = f32[256,128]{1,0:T(8,128)S(1)} all-gather(f32[64,128]{1,0:T(8,128)S(1)} %fusion.27), channel_id=1, replica_groups=mesh['prow'=4,'pcol'=8] {'prow'}, dimensions={0}, use_global_device_ids=true | all-gather | bytes 163840 | tf_op jit(solution)/shard_map/all_gather | solution.py:30
  352.0 5.4 %all_gather.91 = f32[256,128]{1,0:T(8,128)S(1)} all-gather(f32[64,128]{1,0:T(8,128)S(1)} %fusion.29), channel_id=1, replica_groups=mesh['prow'=4,'pcol'=8] {'prow'}, dimensions={0}, use_global_device_ids=true | all-gather | bytes 163840 | tf_op jit(solution)/shard_map/all_gather | solution.py:30
  359.0 5.7 %all_gather.94 = f32[256,128]{1,0:T(8,128)S(1)} all-gather(f32[64,128]{1,0:T(8,128)S(1)} %fusion.31), channel_id=1, replica_groups=mesh['prow'=4,'pcol'=8] {'prow'}, dimensions={0}, use_global_device_ids=true | all-gather | bytes 163840 | tf_op jit(solution)/shard_map/all_gather | solution.py:30
  366.3 5.4 %all_gather.97 = f32[256,128]{1,0:T(8,128)S(1)} all-gather(f32[64,128]{1,0:T(8,128)S(1)} %fusion.33), channel_id=1, replica_groups=mesh['prow'=4,'pcol'=8] {'prow'}, dimensions={0}, use_global_device_ids=true | all-gather | bytes 163840 | tf_op jit(solution)/shard_map/all_gather | solution.py:30
  373.4 5.4 %all_gather.100 = f32[256,128]{1,0:T(8,128)S(1)} all-gather(f32[64,128]{1,0:T(8,128)S(1)} %fusion.35), channel_id=1, replica_groups=mesh['prow'=4,'pcol'=8] {'prow'}, dimensions={0}, use_global_device_ids=true | all-gather | bytes 163840 | tf_op jit(solution)/shard_map/all_gather | solution.py:30
  380.5 5.4 %all_gather.103 = f32[256,128]{1,0:T(8,128)S(1)} all-gather(f32[64,128]{1,0:T(8,128)S(1)} %fusion.37), channel_id=1, replica_groups=mesh['prow'=4,'pcol'=8] {'prow'}, dimensions={0}, use_global_device_ids=true | all-gather | bytes 163840 | tf_op jit(solution)/shard_map/all_gather | solution.py:30
  (49 shorter events, 21.1 us)
Async XLA Ops:
  6.5 318.1 %all-gather.11.cloned.1.call-start = ((), (), s32[]{:S(2)}) async-start(), calls=%async_computation | async-start | bytes 4718592 | tf_op jit(solution)/shard_map/all_gather | solution.py:17
  7.3 324.0 %all-gather.13.cloned.1.call-start = ((), (), s32[]{:S(2)}) async-start(), calls=%async_computation.1 | async-start | bytes 2621440 | tf_op jit(solution)/shard_map/all_gather | solution.py:16
  8.0 10.4 %copy-start = (f32[16128,128]{1,0:T(8,128)S(1)}, f32[16128,128]{1,0:T(8,128)}, u32[]{:S(2)}) copy-start(f32[16128,128]{1,0:T(8,128)} %param.7) | copy-start | bytes 24772612
  285.5 40.3 %copy-start.3 = (f32[8,64,128]{2,1,0:T(8,128)S(1)}, f32[8,64,128]{2,1,0:T(8,128)}, u32[]{:S(2)}) copy-start(f32[8,64,128]{2,1,0:T(8,128)} %param.5) | copy-start | bytes 786436
  331.3 19.5 %copy-start.1 = (f32[8,64,2048]{2,1,0:T(8,128)S(1)}, f32[8,64,2048]{2,1,0:T(8,128)}, u32[]{:S(2)}) copy-start(f32[8,64,2048]{2,1,0:T(8,128)} %all-gather.11.cloned.1.call-done) | copy-start | bytes 12582916
  331.3 26.1 %copy-start.2 = (f32[8,256,256]{2,1,0:T(8,128)S(1)}, f32[8,256,256]{2,1,0:T(8,128)}, u32[]{:S(2)}) copy-start(f32[8,256,256]{2,1,0:T(8,128)} %all-gather.13.cloned.1.call-done) | copy-start | bytes 6291460
Sparse Core Ops, SparseCore 0:
  9.4 83.2 all-gather.10
  94.3 21.2 all-gather.12
